TPU v7x, 512 devices: a whole 4x4x16 slice. The times are simulated.
512 devices in a mesh: site: 64 (over y, z), vec: 8 (over x, core).
Axes of the slice: x: 4, y: 4, z: 16, core: 2. Of those that a mesh axis runs over, the one named last changes fastest.
Arguments:
- diag_blocks: float32 [512, 64, 128], P('site'), as said below
- hop_blocks: float32 [512, 4, 64, 128], P('site'), may hold values from -0.1875 to 0.1875
- neighbors: int32 [512, 8], P('site'), may hold values from 0 to 511, as said below
- start_basis: float32 [512, 128, 512], P('site', None, 'vec'), may hold values from -6 to 6
Outputs:
- basis: float32 [512, 128, 512], P('site', None, 'vec')
- projected: float32 [512, 512], P(None, 'vec')
Inputs may be any that keep to these rules, and one draw needn't show every extreme that they name: neighbors[s, d] is the site one step forward (d = 0, 1, 2, 3 along x, y, z, t) or back (d = 4 + k along the same k) of site s on a periodic 2 x 2 x 2 x 64 lattice; rows j * 8 to (j + 1) * 8 - 1 hold time slice j in an arbitrary order, so the t neighbours lie in the next and previous slice (wrapping) and the others in the same slice. `diag_blocks`: each diagonal block is Hermitian: its left half is symmetric and its right half antisymmetric.
All inputs are finite; a program needn't handle non-finite values.
Results may differ from a plain program's by a relative error of at most 0.00021.
Values sent between devices are 32-bit elements; how exact they have to be, the bound alone decides.
No kernel may reach another device: no remote copies, remote signals or barrier semaphores. Data moves between devices by JAX's collectives and lax.ppermute only.
A program may use at most 64 MiB of HBM per device.

v0:
```python
import jax
import jax.numpy as jnp
from jax import lax
from jax.sharding import PartitionSpec as P

DEGREE = 4
filter_center = 3.7
filter_radius = 3.1
highest = lax.Precision.HIGHEST


def passed_along(x, axis, by):
    size = lax.axis_size(axis)
    return lax.ppermute(x, axis, [(i, (i + by) % size) for i in range(size)])


def embed(weights):
    half_size = weights.shape[-2]
    real_part = weights[..., :half_size]
    imag_part = weights[..., half_size:]
    upper_rows = jnp.concatenate([real_part, -imag_part], -1)
    lower_rows = jnp.concatenate([imag_part, real_part], -1)
    return jnp.concatenate([upper_rows, lower_rows], -2)


def operate(vectors, matrices, pool_index, time_back):
    ahead_block = passed_along(vectors, "site", -1)
    pool = jnp.concatenate([vectors, ahead_block], 0)
    sources = jnp.take(pool, pool_index[:, :8], axis=0)
    summed = jnp.einsum("sjab,sjbc->sac", matrices, sources, precision=highest)
    backward = jnp.einsum("sba,sbc->sac", time_back, vectors, precision=highest)
    backward = passed_along(backward, "site", 1)
    return summed + jnp.take(backward, pool_index[:, 8], axis=0)


def filtered(start_block, operator_apply):
    previous = start_block
    current = (operator_apply(start_block) - filter_center * start_block) / filter_radius
    for order_step in range(DEGREE - 1):
        following = (
            2.0 * (operator_apply(current) - filter_center * current) / filter_radius - previous
        )
        previous, current = (current, following)
    return current


def factor_inverse(gram_matrix):
    lower_factor = jnp.linalg.cholesky(gram_matrix)
    identity = jnp.eye(gram_matrix.shape[0], dtype=jnp.float32)
    return jax.scipy.linalg.solve_triangular(lower_factor, identity, lower=True)


def local(diag_blocks, hop_blocks, neighbors, start_basis):
    site_count = start_basis.shape[0]
    local_cols = start_basis.shape[2]
    all_cols = local_cols * lax.axis_size("vec")
    total_rows = site_count * start_basis.shape[1] * lax.axis_size("site")
    col_start = lax.axis_index("vec") * local_cols
    row_index = neighbors % site_count
    own_index = jnp.arange(site_count, dtype=jnp.int32)
    diag_full = embed(diag_blocks)
    hop_full = embed(hop_blocks)
    back_list = []
    for direction in range(3):
        chosen = jnp.take(hop_full[:, direction], row_index[:, 4 + direction], axis=0)
        back_list.append(jnp.swapaxes(chosen, 1, 2))
    matrices = jnp.stack(
        [diag_full, hop_full[:, 0], hop_full[:, 1], hop_full[:, 2], hop_full[:, 3]] + back_list, 1
    )
    pool_index = jnp.stack(
        [
            own_index,
            row_index[:, 0],
            row_index[:, 1],
            row_index[:, 2],
            row_index[:, 3] + site_count,
            row_index[:, 4],
            row_index[:, 5],
            row_index[:, 6],
            row_index[:, 7],
        ],
        1,
    )
    time_back = hop_full[:, 3]

    def operator_apply(vectors):
        return operate(vectors, matrices, pool_index, time_back)

    basis = start_basis
    filtered_block = filtered(basis, operator_apply)
    everything = lax.all_gather(filtered_block, "vec", axis=2, tiled=True).reshape(-1, all_cols)
    own_block = filtered_block.reshape(-1, local_cols)
    gram_part = jnp.einsum("rc,rk->ck", everything, own_block, precision=highest)
    gram_part = lax.psum(gram_part, "site")
    gram_whole = lax.all_gather(gram_part, "vec", axis=1, tiled=True)
    inverse = factor_inverse(gram_whole / total_rows)
    own_rows = lax.dynamic_slice_in_dim(inverse, col_start, local_cols, 0)
    basis_flat = jnp.einsum("rc,kc->rk", everything, own_rows, precision=highest)
    image_block = operator_apply(basis_flat.reshape(filtered_block.shape)).reshape(-1, local_cols)
    moment = jnp.einsum("rc,rk->ck", everything, image_block, precision=highest)
    moment = lax.psum(moment, "site")
    projected = jnp.dot(inverse, moment, precision=highest) / total_rows
    basis = basis_flat.reshape(filtered_block.shape)
    return (basis, projected)


def solution(mesh):
    placed = (
        P("site", None, None),
        P("site", None, None, None),
        P("site", None),
        P("site", None, "vec"),
    )
    return jax.shard_map(
        local,
        mesh=mesh,
        in_specs=placed,
        out_specs=(P("site", None, "vec"), P(None, "vec")),
        check_vma=False,
    )
```

profile of v0, /device:TPU:2, one launch (start us, length us, event | category | flops | bytes accessed | tf_op | source)
XLA Modules:
  0.0 910.2 jit_solution(3755153946303805086)
XLA Ops:
  7.2 14.0 %collective-permute-start = (f32[8,128,64]{1,2,0:T(8,128)}, f32[8,128,64]{1,2,0:T(8,128)}, u32[]{:S(2)}, u32[]{:S(2)}) collective-permute-start(f32[8,128,64]{1,2,0:T(8,128)} %param.13), channel_id=1, source_target_pairs={{0,504},{8,0},{16,8},{24,16},{32,24},{40,32},{48,40},{56,48},{64,5... | collective-permute-start | bytes 786440 | tf_op jit(solution)/shard_map/ppermute | solution.py:14
  45.6 7.6 broadcast_multiply_fusion.1
  53.2 7.2 collective-permute-start.2
  67.5 7.0 collective-permute-done.3
  76.0 7.6 fusion.61
  86.8 3.9 collective-permute-start.5
  94.0 4.7 collective-permute-done.5
  99.2 7.6 fusion.49
  109.3 3.9 collective-permute-start.7
  117.1 3.9 collective-permute-done.7
  122.6 8.3 fusion.37
  131.0 20.6 %all-gather.3.cloned.1.call-done = f32[8,128,512]{1,2,0:T(8,128)} async-done(((f32[8,128,64]{1,2,0:T(8,128)}), f32[8,128,512]{1,2,0:T(8,128)}) %all-gather.3.cloned.1.call-update) | async-done | bytes 2097168 | tf_op jit(solution)/shard_map/all_gather | solution.py:91
  151.6 4.4 convolution_bitcast_fusion.1
  156.0 262.2 %all-reduce.4.cloned.1.call-done = f32[512,64]{0,1:T(8,128)} async-done(((f32[512,64]{0,1:T(8,128)}), f32[512,64]{0,1:T(8,128)}) %all-reduce.4.cloned.1.call-update) | async-done | bytes 131088 | tf_op jit(solution)/shard_map/psum | solution.py:94
  420.6 23.9 %all-gather.5.cloned.1.call-done = f32[512,512]{0,1:T(8,128)} async-done(((f32[512,64]{0,1:T(8,128)}), f32[512,512]{0,1:T(8,128)}) %all-gather.5.cloned.1.call-update) | async-done | bytes 1048592 | tf_op jit(solution)/shard_map/all_gather | solution.py:95
  452.0 11.7 %cholesky.104 = f32[128,128]{1,0:T(8,128)S(1)} custom-call(f32[128,128]{1,0:T(8,128)S(1)} %cholesky.266), custom_call_target="Cholesky" | custom-call | tf_op jit(solution)/shard_map/jit(cholesky)/cholesky | solution.py:48
  463.9 9.8 %custom-call.31 = f32[1,128,128]{1,2,0:T(8,128)S(1)} custom-call(f32[1,128,128]{2,1,0:T(8,128)S(1)} %get-tuple-element.47), custom_call_target="InvertDiagBlocksLowerTriangular" | custom-call | tf_op jit(solution)/shard_map/jit(cholesky)/cholesky | solution.py:48
  476.2 11.7 %cholesky.217 = f32[128,128]{1,0:T(8,128)S(1)} custom-call(f32[128,128]{1,0:T(8,128)S(1)} %cholesky.270), custom_call_target="Cholesky" | custom-call | tf_op jit(solution)/shard_map/jit(cholesky)/cholesky | solution.py:48
  489.3 9.9 %custom-call.32 = f32[1,128,128]{1,2,0:T(8,128)S(1)} custom-call(f32[1,128,128]{2,1,0:T(8,128)S(1)} %get-tuple-element.44), custom_call_target="InvertDiagBlocksLowerTriangular" | custom-call | tf_op jit(solution)/shard_map/jit(cholesky)/cholesky | solution.py:48
  500.8 11.7 %cholesky.238 = f32[128,128]{1,0:T(8,128)S(1)} custom-call(f32[128,128]{1,0:T(8,128)S(1)} %cholesky.275), custom_call_target="Cholesky" | custom-call | tf_op jit(solution)/shard_map/jit(cholesky)/cholesky | solution.py:48
  513.2 9.8 %custom-call.33 = f32[1,128,128]{1,2,0:T(8,128)S(1)} custom-call(f32[1,128,128]{2,1,0:T(8,128)S(1)} %get-tuple-element.41), custom_call_target="InvertDiagBlocksLowerTriangular" | custom-call | tf_op jit(solution)/shard_map/jit(cholesky)/cholesky | solution.py:48
  524.5 11.9 %cholesky.255 = f32[128,128]{1,0:T(8,128)S(1)} custom-call(f32[128,128]{1,0:T(8,128)S(1)} %convolution_subtract_fusion.5), custom_call_target="Cholesky" | custom-call | tf_op jit(solution)/shard_map/jit(cholesky)/cholesky | solution.py:48
  540.8 14.3 %while.1 = (s32[]{:T(128)}, f32[512,512]{1,0:T(8,128)}, s32[4,2]{0,1:T(2,128)S(1)}, f32[4,128,128]{2,1,0:T(8,128)}, s32[]{:T(128)}) while((s32[]{:T(128)}, f32[512,512]{1,0:T(8,128)}, s32[4,2]{0,1:T(2,128)S(1)}, f32[4,128,128]{2,1,0:T(8,128)}, s32[]{:T(128)}) %tuple.47), condition=%wide.while_cond, body=%wide.while_body.sunk | while | flops 2 | bytes 132705 | solution.py:50
  541.5 2.9 bitcast_dynamic-update-slice_fusion.5
  545.1 2.9 bitcast_dynamic-update-slice_fusion.5
  548.6 2.9 bitcast_dynamic-update-slice_fusion.5
  552.2 2.9 bitcast_dynamic-update-slice_fusion.5
  555.1 40.1 %custom-call.34 = f32[4,128,128]{1,2,0:T(8,128)S(1)} custom-call(f32[4,128,128]{2,1,0:T(8,128)} %get-tuple-element.12), custom_call_target="InvertDiagBlocksLowerTriangular" | custom-call | tf_op jit(solution)/shard_map/jit(_solve_triangular)/triangular_solve | solution.py:50
  604.8 7.7 collective-permute-start.8
  620.5 13.0 %collective-permute-done.9 = f32[8,128,64]{2,1,0:T(8,128)S(1)} collective-permute-done((f32[8,128,64]{2,1,0:T(8,128)}, f32[8,128,64]{2,1,0:T(8,128)S(1)}, u32[]{:S(2)}, u32[]{:S(2)}) %collective-permute-start.9) | collective-permute-done | bytes 262176 | tf_op jit(solution)/shard_map/ppermute | solution.py:14
  634.9 6.8 fusion.13
  644.3 256.3 %all-reduce.6.cloned.1.call-done = f32[512,64]{1,0:T(8,128)} async-done(((f32[512,64]{1,0:T(8,128)}), f32[512,64]{1,0:T(8,128)}) %all-reduce.6.cloned.1.call-update) | async-done | bytes 131088 | tf_op jit(solution)/shard_map/psum | solution.py:101
  (140 shorter events, 93.9 us)
Async XLA Ops:
  7.2 15.2 %copy-start.4 = (f32[8,4,64,128]{3,2,1,0:T(8,128)S(1)}, f32[8,4,64,128]{3,2,1,0:T(8,128)}, u32[]{:S(2)}) copy-start(f32[8,4,64,128]{3,2,1,0:T(8,128)} %param.11) | copy-start | bytes 3145732
  7.2 144.4 %all-gather.3.cloned.1.call-start = ((), (), s32[]{:S(2)}) async-start(), calls=%async_computation | async-start | bytes 2359296 | tf_op jit(solution)/shard_map/all_gather | solution.py:91
  7.2 33.9 %collective-permute-start = (f32[8,128,64]{1,2,0:T(8,128)}, f32[8,128,64]{1,2,0:T(8,128)}, u32[]{:S(2)}, u32[]{:S(2)}) collective-permute-start(f32[8,128,64]{1,2,0:T(8,128)} %param.13), channel_id=1, source_target_pairs={{0,504},{8,0},{16,8},{24,16},{32,24},{40,32},{48,40},{56,48},{64,5... | collective-permute-start | bytes 786440 | tf_op jit(solution)/shard_map/ppermute | solution.py:14
  23.0 1.0 copy-start.5
  23.6 5.1 copy-start
  24.0 4.8 copy-start.10
  25.7 18.3 %collective-permute-start.1 = (f32[8,128,64]{1,2,0:T(8,128)}, f32[8,128,64]{1,2,0:T(8,128)}, u32[]{:S(2)}, u32[]{:S(2)}) collective-permute-start(f32[8,128,64]{1,2,0:T(8,128)} %fusion.94), channel_id=1, source_target_pairs={{0,8},{8,16},{16,24},{24,32},{32,40},{40,48},{48,56},{56,64},{64,7... | collective-permute-start | bytes 786440 | tf_op jit(solution)/shard_map/ppermute | solution.py:14
  38.2 1.9 copy-start.8
  53.2 12.2 %collective-permute-start.2 = (f32[8,128,64]{1,2,0:T(8,128)S(1)}, f32[8,128,64]{1,2,0:T(8,128)S(1)}, u32[]{:S(2)}, u32[]{:S(2)}) collective-permute-start(f32[8,128,64]{1,2,0:T(8,128)S(1)} %get-tuple-element.49), channel_id=1, source_target_pairs={{0,504},{8,0},{16,8},{24,16},{32,24},{40,32},{48,40},{56,48},{64,5... | collective-permute-start | bytes 786440 | tf_op jit(solution)/shard_map/ppermute | solution.py:14
  61.8 12.7 %collective-permute-start.3 = (f32[8,128,64]{1,2,0:T(8,128)}, f32[8,128,64]{1,2,0:T(8,128)}, u32[]{:S(2)}, u32[]{:S(2)}) collective-permute-start(f32[8,128,64]{1,2,0:T(8,128)} %fusion.93), channel_id=1, source_target_pairs={{0,8},{8,16},{16,24},{24,32},{32,40},{40,48},{48,56},{56,64},{64,7... | collective-permute-start | bytes 786440 | tf_op jit(solution)/shard_map/ppermute | solution.py:14
  83.6 8.3 collective-permute-start.4
  86.8 11.8 %collective-permute-start.5 = (f32[8,128,64]{1,2,0:T(8,128)}, f32[8,128,64]{1,2,0:T(8,128)S(1)}, u32[]{:S(2)}, u32[]{:S(2)}) collective-permute-start(f32[8,128,64]{1,2,0:T(8,128)} %fusion.92), channel_id=1, source_target_pairs={{0,8},{8,16},{16,24},{24,32},{32,40},{40,48},{48,56},{56,64},{64,7... | collective-permute-start | bytes 786440 | tf_op jit(solution)/shard_map/ppermute | solution.py:14
  106.8 8.3 collective-permute-start.6
  109.3 11.7 %collective-permute-start.7 = (f32[8,128,64]{1,2,0:T(8,128)S(1)}, f32[8,128,64]{1,2,0:T(8,128)}, u32[]{:S(2)}, u32[]{:S(2)}) collective-permute-start(f32[8,128,64]{1,2,0:T(8,128)S(1)} %fusion.91), channel_id=1, source_target_pairs={{0,8},{8,16},{16,24},{24,32},{32,40},{40,48},{48,56},{56,64},{64,7... | collective-permute-start | bytes 786440 | tf_op jit(solution)/shard_map/ppermute | solution.py:14
  130.9 287.2 %all-reduce.4.cloned.1.call-start = ((), (), s32[]{:S(2)}) async-start(), calls=%async_computation.1 | async-start | bytes 262144 | tf_op jit(solution)/shard_map/psum | solution.py:94
  156.0 288.5 %all-gather.5.cloned.1.call-start = ((), (), s32[]{:S(2)}) async-start(), calls=%async_computation.2 | async-start | bytes 1179648 | tf_op jit(solution)/shard_map/all_gather | solution.py:95
  418.2 482.5 %all-reduce.6.cloned.1.call-start = ((), (), s32[]{:S(2)}) async-start(), calls=%async_computation.3 | async-start | bytes 524288 | tf_op jit(solution)/shard_map/psum | solution.py:101
  444.5 5.0 copy-start.3
  450.9 1.0 copy-start.6
  595.2 4.9 copy-start.9
  600.1 3.2 copy-start.1
  604.8 15.8 %copy-start.7 = (f32[8,128,64]{1,2,0:T(8,128)}, f32[8,128,64]{1,2,0:T(8,128)S(1)}, u32[]{:S(2)}) copy-start(f32[8,128,64]{1,2,0:T(8,128)S(1)} %fusion.106) | copy-start | bytes 786436
  604.8 13.7 %collective-permute-start.8 = (f32[8,128,64]{1,2,0:T(8,128)S(1)}, f32[8,128,64]{1,2,0:T(8,128)S(1)}, u32[]{:S(2)}, u32[]{:S(2)}) collective-permute-start(f32[8,128,64]{1,2,0:T(8,128)S(1)} %fusion.106), channel_id=1, source_target_pairs={{0,504},{8,0},{16,8},{24,16},{32,24},{40,32},{48,40},{56,48},{64,5... | collective-permute-start | bytes 786440 | tf_op jit(solution)/shard_map/ppermute | solution.py:14
  614.3 19.2 %collective-permute-start.9 = (f32[8,128,64]{2,1,0:T(8,128)}, f32[8,128,64]{2,1,0:T(8,128)S(1)}, u32[]{:S(2)}, u32[]{:S(2)}) collective-permute-start(f32[8,128,64]{2,1,0:T(8,128)} %fusion.90), channel_id=1, source_target_pairs={{0,8},{8,16},{16,24},{24,32},{32,40},{40,48},{48,56},{56,64},{64,7... | collective-permute-start | bytes 786440 | tf_op jit(solution)/shard_map/ppermute | solution.py:14
  634.9 6.9 copy-start.2
Sparse Core Ops, SparseCore 0:
  131.0 20.4 all-gather.2
  156.1 262.0 all-reduce.3
  420.3 24.1 all-gather.4
  644.5 256.1 all-reduce.5
where the time goes:
time: 918 us; the launch traced here: 910 us
  waiting for transfers between devices  598 us (65%)
  other arithmetic  133 us (14%)
  matrix products  69.3 us (8%)
  starting transfers between devices  47.3 us (5%)
  local copies, waits for them, and re-layouts  45.1 us (5%)
  between operations  17.2 us (2%)
    psum x1, waiting for transfers between devices, local(): gram_part = lax.psum(gram_part, 'site')  262 us
    psum x1, waiting for transfers between devices, local(): moment = lax.psum(moment, 'site')  256 us
    another operation x15, other arithmetic, factor_inverse(): lower_factor = jnp.linalg.cholesky(gram_matrix)  79.4 us
    ppermute x10, starting transfers between devices, passed_along(): return lax.ppermute(x, axis, [(i, (i + by) % size) for i in range(size)])  46.7 us
    another operation x4, other arithmetic, factor_inverse(): return jax.scipy.linalg.solve_triangular(lower_factor, identity, lower=True)  41.3 us
    dot_general x5, matrix products, operate(): summed = jnp.einsum('sjab,sjbc->sac', matrices, sources, precision=highest)  38.1 us
    ppermute x10, waiting for transfers between devices, passed_along(): return lax.ppermute(x, axis, [(i, (i + by) % size) for i in range(size)])  35.1 us
    all_gather x1, waiting for transfers between devices, local(): gram_whole = lax.all_gather(gram_part, 'vec', axis=1, tiled=True)  23.9 us
  transfers between devices with their start and end apart: 14, of which 12 were waited for; matrix products, arithmetic and copies ran while one was open for 4% of the time, Pallas kernels for 0%

commit v1 on v0

--- a/solution.py
+++ b/solution.py
@@ -91,7 +91,7 @@
     everything = lax.all_gather(filtered_block, "vec", axis=2, tiled=True).reshape(-1, all_cols)
     own_block = filtered_block.reshape(-1, local_cols)
     gram_part = jnp.einsum("rc,rk->ck", everything, own_block, precision=highest)
-    gram_part = lax.psum(gram_part, "site")
+    gram_part = jnp.sum(lax.all_gather(gram_part, "site"), axis=0)
     gram_whole = lax.all_gather(gram_part, "vec", axis=1, tiled=True)
     inverse = factor_inverse(gram_whole / total_rows)
     own_rows = lax.dynamic_slice_in_dim(inverse, col_start, local_cols, 0)

time: 918 us -> 824 us (0.90)
  waiting for transfers between devices: 598 us -> 493 us
    psum x1 -> x0, waiting for transfers between devices: 262 us -> none  [local(): gram_part = lax.psum(gram_part, 'site')]
    all_gather x0 -> x1, waiting for transfers between devices: none -> 159 us  [local(): gram_part = jnp.sum(lax.all_gather(gram_part, 'site'), axis=0)]
where the time goes in v1:
time: 824 us; the launch traced here: 817 us
  waiting for transfers between devices  493 us (60%)
  other arithmetic  136 us (17%)
  matrix products  69.2 us (8%)
  local copies, waits for them, and re-layouts  53.4 us (6%)
  starting transfers between devices  47.8 us (6%)
  between operations  17.3 us (2%)
    psum x1, waiting for transfers between devices, local(): moment = lax.psum(moment, 'site')  257 us
    all_gather x1, waiting for transfers between devices, local(): gram_part = jnp.sum(lax.all_gather(gram_part, 'site'), axis=0)  159 us
    another operation x15, other arithmetic, factor_inverse(): lower_factor = jnp.linalg.cholesky(gram_matrix)  79.4 us
    ppermute x10, starting transfers between devices, passed_along(): return lax.ppermute(x, axis, [(i, (i + by) % size) for i in range(size)])  47.2 us
    another operation x4, other arithmetic, factor_inverse(): return jax.scipy.linalg.solve_triangular(lower_factor, identity, lower=True)  41.4 us
    dot_general x5, matrix products, operate(): summed = jnp.einsum('sjab,sjbc->sac', matrices, sources, precision=highest)  38.1 us
    ppermute x10, waiting for transfers between devices, passed_along(): return lax.ppermute(x, axis, [(i, (i + by) % size) for i in range(size)])  34.5 us
    all_gather x1, waiting for transfers between devices, local(): gram_whole = lax.all_gather(gram_part, 'vec', axis=1, tiled=True)  22.4 us
  transfers between devices with their start and end apart: 14, of which 12 were waited for; matrix products, arithmetic and copies ran while one was open for 4% of the time, Pallas kernels for 0%

profile of v1, /device:TPU:2, one launch (start us, length us, event | category | flops | bytes accessed | tf_op | source)
XLA Modules:
  0.0 816.8 jit_solution(16095290115614211450)
XLA Ops:
  7.2 14.0 %collective-permute-start = (f32[8,128,64]{1,2,0:T(8,128)}, f32[8,128,64]{1,2,0:T(8,128)}, u32[]{:S(2)}, u32[]{:S(2)}) collective-permute-start(f32[8,128,64]{1,2,0:T(8,128)} %param.13), channel_id=1, source_target_pairs={{0,504},{8,0},{16,8},{24,16},{32,24},{40,32},{48,40},{56,48},{64,5... | collective-permute-start | bytes 786440 | tf_op jit(solution)/shard_map/ppermute | solution.py:14
  45.6 7.6 broadcast_multiply_fusion.1
  53.3 7.2 collective-permute-start.2
  67.6 7.0 collective-permute-done.3
  76.0 7.6 fusion.61
  86.9 3.9 collective-permute-start.5
  94.0 4.6 collective-permute-done.5
  99.2 7.6 fusion.49
  109.4 4.1 collective-permute-start.7
  117.2 3.9 collective-permute-done.7
  122.6 8.3 %fusion.37 = f32[8,128,64]{1,2,0:T(8,128)} fusion(f32[8,128,64]{1,2,0:T(8,128)S(1)} %fusion.61, f32[8,8,128,128]{3,2,1,0:T(8,128)} %bitcast_dynamic-update-slice_fusion.1, f32[8,8,128,64]{2,3,1,0:T(8,128)} %bitcast.157, pred[8,8]{1,0:T(8,128)(4,1)S(1)} %compare_and_fusion, f32[8,128,64]{1,2,0:T(8,128)S(1)} %gather_fusion.10, f32[8,128,64]{1,2,0:T(8,128)S(1)} %fusion.49, ...), kind=kOutput, calls=%fused_computation.41 | convolution fusion | flops 806223872 | bytes 7340104 | tf_op jit(solution)/shard_map/sjab,sjbc->sac/dot_general | solution.py:30
  131.0 20.6 %all-gather.5.cloned.1.call-done = f32[8,128,512]{1,2,0:T(8,128)} async-done(((f32[8,128,64]{1,2,0:T(8,128)}), f32[8,128,512]{1,2,0:T(8,128)}) %all-gather.5.cloned.1.call-update) | async-done | bytes 2097168 | tf_op jit(solution)/shard_map/all_gather | solution.py:91
  151.6 4.4 convolution_bitcast_fusion.1
  156.0 158.8 %all-gather.9.cloned.1.call-done = f32[32768,64]{0,1:T(8,128)} async-done(((f32[512,64]{0,1:T(8,128)}), f32[32768,64]{0,1:T(8,128)}) %all-gather.9.cloned.1.call-update) | async-done | bytes 8388624 | tf_op jit(solution)/shard_map/all_gather | solution.py:94
  314.8 8.1 copy.16
  323.0 3.1 bitcast_reduce_fusion
  328.4 22.4 %all-gather.7.cloned.1.call-done = f32[512,512]{0,1:T(8,128)} async-done(((f32[512,64]{0,1:T(8,128)}), f32[512,512]{0,1:T(8,128)}) %all-gather.7.cloned.1.call-update) | async-done | bytes 1048592 | tf_op jit(solution)/shard_map/all_gather | solution.py:95
  358.2 11.7 %cholesky.104 = f32[128,128]{1,0:T(8,128)S(1)} custom-call(f32[128,128]{1,0:T(8,128)S(1)} %cholesky.266), custom_call_target="Cholesky" | custom-call | tf_op jit(solution)/shard_map/jit(cholesky)/cholesky | solution.py:48
  370.1 9.8 %custom-call.31 = f32[1,128,128]{1,2,0:T(8,128)S(1)} custom-call(f32[1,128,128]{2,1,0:T(8,128)S(1)} %get-tuple-element.47), custom_call_target="InvertDiagBlocksLowerTriangular" | custom-call | tf_op jit(solution)/shard_map/jit(cholesky)/cholesky | solution.py:48
  382.4 11.7 %cholesky.217 = f32[128,128]{1,0:T(8,128)S(1)} custom-call(f32[128,128]{1,0:T(8,128)S(1)} %cholesky.270), custom_call_target="Cholesky" | custom-call | tf_op jit(solution)/shard_map/jit(cholesky)/cholesky | solution.py:48
  395.5 9.9 %custom-call.32 = f32[1,128,128]{1,2,0:T(8,128)S(1)} custom-call(f32[1,128,128]{2,1,0:T(8,128)S(1)} %get-tuple-element.44), custom_call_target="InvertDiagBlocksLowerTriangular" | custom-call | tf_op jit(solution)/shard_map/jit(cholesky)/cholesky | solution.py:48
  407.0 11.7 %cholesky.238 = f32[128,128]{1,0:T(8,128)S(1)} custom-call(f32[128,128]{1,0:T(8,128)S(1)} %cholesky.275), custom_call_target="Cholesky" | custom-call | tf_op jit(solution)/shard_map/jit(cholesky)/cholesky | solution.py:48
  419.5 9.8 %custom-call.33 = f32[1,128,128]{1,2,0:T(8,128)S(1)} custom-call(f32[1,128,128]{2,1,0:T(8,128)S(1)} %get-tuple-element.41), custom_call_target="InvertDiagBlocksLowerTriangular" | custom-call | tf_op jit(solution)/shard_map/jit(cholesky)/cholesky | solution.py:48
  430.7 11.9 %cholesky.255 = f32[128,128]{1,0:T(8,128)S(1)} custom-call(f32[128,128]{1,0:T(8,128)S(1)} %convolution_subtract_fusion.5), custom_call_target="Cholesky" | custom-call | tf_op jit(solution)/shard_map/jit(cholesky)/cholesky | solution.py:48
  447.2 14.4 %while.1 = (s32[]{:T(128)}, f32[512,512]{1,0:T(8,128)}, s32[4,2]{0,1:T(2,128)S(1)}, f32[4,128,128]{2,1,0:T(8,128)}, s32[]{:T(128)}) while((s32[]{:T(128)}, f32[512,512]{1,0:T(8,128)}, s32[4,2]{0,1:T(2,128)S(1)}, f32[4,128,128]{2,1,0:T(8,128)}, s32[]{:T(128)}) %tuple.47), condition=%wide.while_cond, body=%wide.while_body.sunk | while | flops 2 | bytes 132705 | solution.py:50
  447.8 3.0 bitcast_dynamic-update-slice_fusion.5
  451.4 3.0 bitcast_dynamic-update-slice_fusion.5
  461.5 40.1 %custom-call.34 = f32[4,128,128]{1,2,0:T(8,128)S(1)} custom-call(f32[4,128,128]{2,1,0:T(8,128)} %get-tuple-element.12), custom_call_target="InvertDiagBlocksLowerTriangular" | custom-call | tf_op jit(solution)/shard_map/jit(_solve_triangular)/triangular_solve | solution.py:50
  511.2 7.7 collective-permute-start.8
  527.0 13.0 %collective-permute-done.9 = f32[8,128,64]{2,1,0:T(8,128)S(1)} collective-permute-done((f32[8,128,64]{2,1,0:T(8,128)}, f32[8,128,64]{2,1,0:T(8,128)S(1)}, u32[]{:S(2)}, u32[]{:S(2)}) %collective-permute-start.9) | collective-permute-done | bytes 262176 | tf_op jit(solution)/shard_map/ppermute | solution.py:14
  541.3 6.8 fusion.13
  550.7 256.5 %all-reduce.3.cloned.1.call-done = f32[512,64]{1,0:T(8,128)} async-done(((f32[512,64]{1,0:T(8,128)}), f32[512,64]{1,0:T(8,128)}) %all-reduce.3.cloned.1.call-update) | async-done | bytes 131088 | tf_op jit(solution)/shard_map/psum | solution.py:101
  (142 shorter events, 99.7 us)
Async XLA Ops:
  7.2 15.2 %copy-start.4 = (f32[8,4,64,128]{3,2,1,0:T(8,128)S(1)}, f32[8,4,64,128]{3,2,1,0:T(8,128)}, u32[]{:S(2)}) copy-start(f32[8,4,64,128]{3,2,1,0:T(8,128)} %param.11) | copy-start | bytes 3145732
  7.2 144.4 %all-gather.5.cloned.1.call-start = ((), (), s32[]{:S(2)}) async-start(), calls=%async_computation | async-start | bytes 2359296 | tf_op jit(solution)/shard_map/all_gather | solution.py:91
  7.2 33.8 %collective-permute-start = (f32[8,128,64]{1,2,0:T(8,128)}, f32[8,128,64]{1,2,0:T(8,128)}, u32[]{:S(2)}, u32[]{:S(2)}) collective-permute-start(f32[8,128,64]{1,2,0:T(8,128)} %param.13), channel_id=1, source_target_pairs={{0,504},{8,0},{16,8},{24,16},{32,24},{40,32},{48,40},{56,48},{64,5... | collective-permute-start | bytes 786440 | tf_op jit(solution)/shard_map/ppermute | solution.py:14
  23.0 1.0 copy-start.5
  23.6 5.1 copy-start
  24.0 4.8 copy-start.10
  25.7 18.4 %collective-permute-start.1 = (f32[8,128,64]{1,2,0:T(8,128)}, f32[8,128,64]{1,2,0:T(8,128)}, u32[]{:S(2)}, u32[]{:S(2)}) collective-permute-start(f32[8,128,64]{1,2,0:T(8,128)} %fusion.94), channel_id=1, source_target_pairs={{0,8},{8,16},{16,24},{24,32},{32,40},{40,48},{48,56},{56,64},{64,7... | collective-permute-start | bytes 786440 | tf_op jit(solution)/shard_map/ppermute | solution.py:14
  38.2 1.9 copy-start.8
  53.3 12.2 %collective-permute-start.2 = (f32[8,128,64]{1,2,0:T(8,128)S(1)}, f32[8,128,64]{1,2,0:T(8,128)S(1)}, u32[]{:S(2)}, u32[]{:S(2)}) collective-permute-start(f32[8,128,64]{1,2,0:T(8,128)S(1)} %get-tuple-element.49), channel_id=1, source_target_pairs={{0,504},{8,0},{16,8},{24,16},{32,24},{40,32},{48,40},{56,48},{64,5... | collective-permute-start | bytes 786440 | tf_op jit(solution)/shard_map/ppermute | solution.py:14
  61.8 12.7 %collective-permute-start.3 = (f32[8,128,64]{1,2,0:T(8,128)}, f32[8,128,64]{1,2,0:T(8,128)}, u32[]{:S(2)}, u32[]{:S(2)}) collective-permute-start(f32[8,128,64]{1,2,0:T(8,128)} %fusion.93), channel_id=1, source_target_pairs={{0,8},{8,16},{16,24},{24,32},{32,40},{40,48},{48,56},{56,64},{64,7... | collective-permute-start | bytes 786440 | tf_op jit(solution)/shard_map/ppermute | solution.py:14
  83.7 8.3 %collective-permute-start.4 = (f32[8,128,64]{1,2,0:T(8,128)S(1)}, f32[8,128,64]{1,2,0:T(8,128)S(1)}, u32[]{:S(2)}, u32[]{:S(2)}) collective-permute-start(f32[8,128,64]{1,2,0:T(8,128)S(1)} %fusion.61), channel_id=1, source_target_pairs={{0,504},{8,0},{16,8},{24,16},{32,24},{40,32},{48,40},{56,48},{64,5... | collective-permute-start | bytes 786440 | tf_op jit(solution)/shard_map/ppermute | solution.py:14
  86.9 11.8 %collective-permute-start.5 = (f32[8,128,64]{1,2,0:T(8,128)}, f32[8,128,64]{1,2,0:T(8,128)S(1)}, u32[]{:S(2)}, u32[]{:S(2)}) collective-permute-start(f32[8,128,64]{1,2,0:T(8,128)} %fusion.92), channel_id=1, source_target_pairs={{0,8},{8,16},{16,24},{24,32},{32,40},{40,48},{48,56},{56,64},{64,7... | collective-permute-start | bytes 786440 | tf_op jit(solution)/shard_map/ppermute | solution.py:14
  106.9 8.3 %collective-permute-start.6 = (f32[8,128,64]{1,2,0:T(8,128)S(1)}, f32[8,128,64]{1,2,0:T(8,128)S(1)}, u32[]{:S(2)}, u32[]{:S(2)}) collective-permute-start(f32[8,128,64]{1,2,0:T(8,128)S(1)} %fusion.49), channel_id=1, source_target_pairs={{0,504},{8,0},{16,8},{24,16},{32,24},{40,32},{48,40},{56,48},{64,5... | collective-permute-start | bytes 786440 | tf_op jit(solution)/shard_map/ppermute | solution.py:14
  109.4 11.7 %collective-permute-start.7 = (f32[8,128,64]{1,2,0:T(8,128)S(1)}, f32[8,128,64]{1,2,0:T(8,128)}, u32[]{:S(2)}, u32[]{:S(2)}) collective-permute-start(f32[8,128,64]{1,2,0:T(8,128)S(1)} %fusion.91), channel_id=1, source_target_pairs={{0,8},{8,16},{16,24},{24,32},{32,40},{40,48},{48,56},{56,64},{64,7... | collective-permute-start | bytes 786440 | tf_op jit(solution)/shard_map/ppermute | solution.py:14
  131.0 183.9 %all-gather.9.cloned.1.call-start = ((), (), s32[]{:S(2)}) async-start(), calls=%async_computation.3 | async-start | bytes 8519680 | tf_op jit(solution)/shard_map/all_gather | solution.py:94
  156.0 194.8 %all-gather.7.cloned.1.call-start = ((), (), s32[]{:S(2)}) async-start(), calls=%async_computation.1 | async-start | bytes 1179648 | tf_op jit(solution)/shard_map/all_gather | solution.py:95
  326.0 481.2 %all-reduce.3.cloned.1.call-start = ((), (), s32[]{:S(2)}) async-start(), calls=%async_computation.2 | async-start | bytes 524288 | tf_op jit(solution)/shard_map/psum | solution.py:101
  350.8 5.0 copy-start.3
  357.2 1.0 copy-start.6
  501.7 4.9 copy-start.9
  506.5 3.2 copy-start.1
  511.2 15.8 %copy-start.7 = (f32[8,128,64]{1,2,0:T(8,128)}, f32[8,128,64]{1,2,0:T(8,128)S(1)}, u32[]{:S(2)}) copy-start(f32[8,128,64]{1,2,0:T(8,128)S(1)} %fusion.106) | copy-start | bytes 786436
  511.2 13.7 %collective-permute-start.8 = (f32[8,128,64]{1,2,0:T(8,128)S(1)}, f32[8,128,64]{1,2,0:T(8,128)S(1)}, u32[]{:S(2)}, u32[]{:S(2)}) collective-permute-start(f32[8,128,64]{1,2,0:T(8,128)S(1)} %fusion.106), channel_id=1, source_target_pairs={{0,504},{8,0},{16,8},{24,16},{32,24},{40,32},{48,40},{56,48},{64,5... | collective-permute-start | bytes 786440 | tf_op jit(solution)/shard_map/ppermute | solution.py:14
  520.7 19.2 %collective-permute-start.9 = (f32[8,128,64]{2,1,0:T(8,128)}, f32[8,128,64]{2,1,0:T(8,128)S(1)}, u32[]{:S(2)}, u32[]{:S(2)}) collective-permute-start(f32[8,128,64]{2,1,0:T(8,128)} %fusion.90), channel_id=1, source_target_pairs={{0,8},{8,16},{16,24},{24,32},{32,40},{40,48},{48,56},{56,64},{64,7... | collective-permute-start | bytes 786440 | tf_op jit(solution)/shard_map/ppermute | solution.py:14
  541.3 6.9 copy-start.2
Sparse Core Ops, SparseCore 0:
  131.1 20.4 all-gather.4
  156.1 158.6 all-gather.8
  326.2 24.5 all-gather.6
  550.8 256.3 all-reduce.2
